TPU v7x, 32 devices: a whole 2x2x4 slice. The times are simulated.
32 devices in a mesh: dp: 8 (over y, x, core), tensor: 4 (over z).
Axes of the slice: x: 2, y: 2, z: 4, core: 2. Of those that a mesh axis runs over, the one named last changes fastest.
Arguments:
- hidden: bfloat16 [16384, 768], P('dp'), may hold values from -6 to 6
- teacher: float32 [16384, 768], P('dp'), may hold values from -6 to 6
- valid: int32 [8, 2048], P('dp'), may hold values from 0 to 1, as said below
- w_qkv: bfloat16 [3, 768, 768], P(None, None, 'tensor'), may hold values from -0.21875 to 0.21875
- b_qv: float32 [2, 768], P(None, 'tensor'), may hold values from -1 to 1
- w_attn_out: bfloat16 [768, 768], P('tensor'), may hold values from -1.25 to 1.25
- b_attn_out: float32 [768], replicated, may hold values from -1.5 to 1.5
- gain_one: float32 [768], replicated, may hold values from 0.5 to 1.5
- bias_one: float32 [768], replicated, may hold values from -1.5 to 1.5
- w_up: bfloat16 [768, 3072], P(None, 'tensor'), may hold values from -0.21875 to 0.21875
- b_up: float32 [3072], P('tensor'), may hold values from -2.5 to 2.5
- w_down: bfloat16 [3072, 768], P('tensor'), may hold values from -0.109375 to 0.109375
- b_down: float32 [768], replicated, may hold values from -1.5 to 1.5
- gain_two: float32 [768], replicated, may hold values from 0.5 to 1.5
- bias_two: float32 [768], replicated, may hold values from -1.5 to 1.5
- pairwise_gate_odds_table: float32 [12, 512, 512], P('tensor'), may hold values from -5 to 5
- gate_random_perturbation: float32 [12, 512, 512], P('tensor'), may hold values from -2 to 2
Outputs:
- out_states: float32 [16384, 768], P('dp')
- loss: float32 [], replicated
- grad_hidden: float32 [16384, 768], P('dp')
- grad_w_qkv: float32 [3, 768, 768], P(None, None, 'tensor')
- grad_b_qv: float32 [2, 768], P(None, 'tensor')
- grad_w_attn_out: float32 [768, 768], P('tensor')
- grad_b_attn_out: float32 [768], replicated
- grad_gain_one: float32 [768], replicated
- derivative_first_offset: float32 [768], replicated
- grad_w_up: float32 [768, 3072], P(None, 'tensor')
- grad_b_up: float32 [3072], P('tensor')
- grad_w_down: float32 [3072, 768], P('tensor')
- grad_b_down: float32 [768], replicated
- grad_gain_two: float32 [768], replicated
- grad_bias_two: float32 [768], replicated
- grad_mask_logits: float32 [12, 512, 512], P('tensor')
Inputs may be any that keep to these rules, and one draw needn't show every extreme that they name: The first token of every sequence is valid.
All inputs are finite; a program needn't handle non-finite values.
Results may differ from a plain program's by a relative error of at most 0.019.
Values may be sent and summed in bfloat16 or wider, within the bound.
No kernel may reach another device: no remote copies, remote signals or barrier semaphores. Data moves between devices by JAX's collectives and lax.ppermute only.
A program may use at most 256 MiB of HBM per device.

v0:
```python
import math
import jax
import jax.numpy as jnp
from jax import lax
from jax.sharding import PartitionSpec as P

BLOCK = 256
epsilon = 1e-06
gumbel_softening_factor = 0.5


def normed(resid, gain, shift):
    average = jnp.mean(resid, axis=-1, keepdims=True)
    centred = resid - average
    variance = jnp.mean(centred * centred, axis=-1, keepdims=True)
    return centred * lax.rsqrt(variance + epsilon) * gain + shift


def exact_gelu(inputs):
    return jax.nn.gelu(inputs, approximate=False)


def block_scores(queries, key_vectors, gate_natural_log, block_index, score_scale):
    period = gate_natural_log.shape[1]
    head_count = gate_natural_log.shape[0]
    head_width = queries.shape[1] // head_count
    key_span = (block_index + 1) * period
    query_rows = queries[block_index * period : key_span].reshape(period, head_count, head_width)
    key_row_block = key_vectors[:key_span].reshape(key_span, head_count, head_width)
    scores = (
        jnp.einsum("qhd,khd->hqk", query_rows, key_row_block, preferred_element_type=jnp.float32)
        * score_scale
    )
    scores = scores + jnp.tile(gate_natural_log, (1, 1, block_index + 1))
    row_pos = lax.broadcasted_iota(jnp.int32, (period, key_span), 0) + block_index * period
    col_pos = lax.broadcasted_iota(jnp.int32, (period, key_span), 1)
    allowed = col_pos // BLOCK <= row_pos // BLOCK
    return jnp.where(allowed[None], scores, -1e30)


def body(
    hidden,
    teacher,
    valid,
    w_qkv,
    b_qv,
    w_attn_out,
    b_attn_out,
    gain_one,
    bias_one,
    w_up,
    b_up,
    w_down,
    b_down,
    gain_two,
    bias_two,
    pairwise_gate_odds_table,
    gate_random_perturbation,
):
    seq_tokens = hidden.shape[0]
    model_width = hidden.shape[1]
    period = pairwise_gate_odds_table.shape[1]
    head_count = pairwise_gate_odds_table.shape[0]
    local_width = w_qkv.shape[2]
    head_width = local_width // head_count
    score_scale = 1.0 / math.sqrt(head_width)
    num_blocks = seq_tokens // period
    projected = jnp.einsum("td,kde->kte", hidden, w_qkv, preferred_element_type=jnp.float32)
    queries = (projected[0] + b_qv[0]).astype(jnp.bfloat16)
    key_vectors = projected[1].astype(jnp.bfloat16)
    values = (projected[2] + b_qv[1]).astype(jnp.bfloat16)

    def soft_mask(affinity_preactivations):
        return jax.nn.log_sigmoid(
            (affinity_preactivations + gate_random_perturbation) / gumbel_softening_factor
        )

    gate_natural_log, mask_pull = jax.vjp(soft_mask, pairwise_gate_odds_table)
    contexts = []
    logarithm_sums = []
    for block_index in range(num_blocks):
        scores = block_scores(queries, key_vectors, gate_natural_log, block_index, score_scale)
        highest = jnp.max(scores, axis=-1, keepdims=True)
        exponent = jnp.exp(scores - highest)
        totals = jnp.sum(exponent, axis=-1, keepdims=True)
        soft_weights = (exponent / totals).astype(jnp.bfloat16)
        logarithm_sums.append(highest + jnp.log(totals))
        key_span = (block_index + 1) * period
        value_rows = values[:key_span].reshape(key_span, head_count, head_width)
        contexts.append(
            jnp.einsum("hqk,khd->qhd", soft_weights, value_rows, preferred_element_type=jnp.float32)
        )
    context = (
        jnp.concatenate(contexts, axis=0).reshape(seq_tokens, local_width).astype(jnp.bfloat16)
    )
    hidden_wide = hidden.astype(jnp.float32)
    attn_part = jnp.dot(context, w_attn_out, preferred_element_type=jnp.float32)
    attention = lax.psum(attn_part.astype(jnp.bfloat16), "tensor").astype(jnp.float32) + b_attn_out
    first, first_pull = jax.vjp(normed, hidden_wide + attention, gain_one, bias_one)
    first_low = first.astype(jnp.bfloat16)
    before = jnp.dot(first_low, w_up, preferred_element_type=jnp.float32) + b_up
    activated, gelu_pull = jax.vjp(exact_gelu, before)
    act_low = activated.astype(jnp.bfloat16)
    ffn_part = jnp.dot(act_low, w_down, preferred_element_type=jnp.float32)
    feedforward = lax.psum(ffn_part.astype(jnp.bfloat16), "tensor").astype(jnp.float32) + b_down
    out_states, second_pull = jax.vjp(normed, first + feedforward, gain_two, bias_two)
    valid_rows = valid[0].astype(jnp.float32)[:, None]
    residue = out_states - teacher
    local_error = jnp.sum(valid_rows * residue * residue)
    local_count = jnp.sum(valid_rows)
    total_valid, total_error = lax.psum((local_count, local_error), "dp")
    loss_value = total_error / (total_valid * model_width)
    factor = seq_tokens / total_valid
    upstream_derivative = 2.0 * factor * valid_rows * residue
    grad_second, grad_gain_two, grad_bias_two = second_pull(upstream_derivative)
    grad_ffn = grad_second.astype(jnp.bfloat16)
    grad_b_down = jnp.sum(grad_ffn, axis=0, dtype=jnp.float32)
    grad_w_down = jnp.einsum("tf,td->fd", act_low, grad_ffn, preferred_element_type=jnp.float32)
    grad_act = jnp.einsum("td,fd->tf", grad_ffn, w_down, preferred_element_type=jnp.float32)
    grad_before = gelu_pull(grad_act)[0].astype(jnp.bfloat16)
    grad_b_up = jnp.sum(grad_before, axis=0, dtype=jnp.float32)
    grad_w_up = jnp.einsum("td,tf->df", first_low, grad_before, preferred_element_type=jnp.float32)
    back_first = jnp.einsum("tf,df->td", grad_before, w_up, preferred_element_type=jnp.float32)
    grad_first = grad_second + lax.psum(back_first.astype(jnp.bfloat16), "tensor").astype(
        jnp.float32
    )
    grad_resid, grad_gain_one, derivative_first_offset = first_pull(grad_first)
    grad_attn = grad_resid.astype(jnp.bfloat16)
    grad_b_attn_out = jnp.sum(grad_attn, axis=0, dtype=jnp.float32)
    grad_w_attn_out = jnp.einsum(
        "tc,td->cd", context, grad_attn, preferred_element_type=jnp.float32
    )
    grad_context = jnp.einsum(
        "td,cd->tc", grad_attn, w_attn_out, preferred_element_type=jnp.float32
    ).astype(jnp.bfloat16)
    grad_queries = []
    grad_keys = jnp.zeros((seq_tokens, head_count, head_width), jnp.float32)
    grad_values = jnp.zeros((seq_tokens, head_count, head_width), jnp.float32)
    grad_log_mask = jnp.zeros(gate_natural_log.shape, jnp.float32)
    for block_index in range(num_blocks):
        scores = block_scores(queries, key_vectors, gate_natural_log, block_index, score_scale)
        soft = jnp.exp(scores - logarithm_sums[block_index])
        start_row = block_index * period
        key_span = start_row + period
        grad_rows = grad_context[start_row:key_span].reshape(period, head_count, head_width)
        query_rows = queries[start_row:key_span].reshape(period, head_count, head_width)
        key_row_block = key_vectors[:key_span].reshape(key_span, head_count, head_width)
        value_rows = values[:key_span].reshape(key_span, head_count, head_width)
        grad_soft = jnp.einsum(
            "qhd,khd->hqk", grad_rows, value_rows, preferred_element_type=jnp.float32
        )
        inner = jnp.sum(soft * grad_soft, axis=-1, keepdims=True)
        grad_scores = (soft * (grad_soft - inner)).astype(jnp.bfloat16)
        grad_log_mask = grad_log_mask + jnp.sum(
            grad_scores.reshape(head_count, period, block_index + 1, period),
            axis=2,
            dtype=jnp.float32,
        )
        grad_queries.append(
            jnp.einsum(
                "hqk,khd->qhd", grad_scores, key_row_block, preferred_element_type=jnp.float32
            )
            * score_scale
        )
        grad_keys = grad_keys.at[:key_span].add(
            jnp.einsum("hqk,qhd->khd", grad_scores, query_rows, preferred_element_type=jnp.float32)
            * score_scale
        )
        grad_values = grad_values.at[:key_span].add(
            jnp.einsum(
                "hqk,qhd->khd",
                soft.astype(jnp.bfloat16),
                grad_rows,
                preferred_element_type=jnp.float32,
            )
        )
    grad_qkv = jnp.stack(
        [
            jnp.concatenate(grad_queries, axis=0).reshape(seq_tokens, local_width),
            grad_keys.reshape(seq_tokens, local_width),
            grad_values.reshape(seq_tokens, local_width),
        ]
    ).astype(jnp.bfloat16)
    grad_w_qkv = jnp.einsum("td,kte->kde", hidden, grad_qkv, preferred_element_type=jnp.float32)
    grad_b_qv = jnp.sum(grad_qkv[0::2], axis=1, dtype=jnp.float32)
    back_hidden = jnp.einsum("kte,kde->td", grad_qkv, w_qkv, preferred_element_type=jnp.float32)
    grad_hidden = grad_resid + lax.psum(back_hidden.astype(jnp.bfloat16), "tensor").astype(
        jnp.float32
    )
    mask_gradient = mask_pull(grad_log_mask)[0]
    summed = lax.psum(
        (
            grad_w_qkv,
            grad_b_qv,
            grad_w_attn_out,
            grad_b_attn_out,
            grad_gain_one,
            derivative_first_offset,
            grad_w_up,
            grad_b_up,
            grad_w_down,
            grad_b_down,
            grad_gain_two,
            grad_bias_two,
            mask_gradient,
        ),
        "dp",
    )
    return (
        out_states,
        loss_value,
        grad_hidden,
        summed[0],
        summed[1],
        summed[2],
        summed[3],
        summed[4],
        summed[5],
        summed[6],
        summed[7],
        summed[8],
        summed[9],
        summed[10],
        summed[11],
        summed[12],
    )


def solution(mesh):
    placed = (
        P("dp", None),
        P("dp", None),
        P("dp", None),
        P(None, None, "tensor"),
        P(None, "tensor"),
        P("tensor", None),
        P(),
        P(),
        P(),
        P(None, "tensor"),
        P("tensor"),
        P("tensor", None),
        P(),
        P(),
        P(),
        P("tensor", None, None),
        P("tensor", None, None),
    )
    return jax.shard_map(
        body,
        mesh=mesh,
        in_specs=placed,
        out_specs=(
            P("dp", None),
            P(),
            P("dp", None),
            P(None, None, "tensor"),
            P(None, "tensor"),
            P("tensor", None),
            P(),
            P(),
            P(),
            P(None, "tensor"),
            P("tensor"),
            P("tensor", None),
            P(),
            P(),
            P(),
            P("tensor", None, None),
        ),
        check_vma=False,
    )
```

profile of v0, /device:TPU:0, one launch (start us, length us, event | category | flops | bytes accessed | tf_op | source)
XLA Modules:
  0.0 1031.9 jit_solution(5200982813277051562)
XLA Ops:
  15.1 4.2 convolution_bitcast_fusion
  26.7 3.5 copy.54
  30.2 3.6 copy.55
  33.8 6.4 fusion.35
  40.2 3.6 copy.57
  46.0 7.0 tile.14
  53.0 9.6 copy.58
  62.6 6.6 tile.12
  69.1 9.2 tile.13
  78.3 7.7 tile.16
  86.1 15.9 %tile.17 = f32[3,512,2048]{2,1,0:T(8,128)} reshape(f32[3,512,4,512]{3,2,1,0:T(4,128)} %tile.16) | data formatting | bytes 25165824 | tf_op jit(solution)/shard_map/tile | solution.py:34
  126.1 6.7 fusion.143
  137.5 3.2 fusion.97
  144.6 123.8 %all-reduce.10.cloned.1.call-done = bf16[2048,768]{1,0:T(8,128)(2,1)} async-done(((bf16[2048,768]{1,0:T(8,128)(2,1)}), bf16[2048,768]{1,0:T(8,128)(2,1)}) %all-reduce.10.cloned.1.call-update) | async-done | bytes 3145744 | tf_op jit(solution)/shard_map/psum | solution.py:98
  268.4 4.1 fusion.17
  274.9 18.6 %multiply_convert_fusion.3 = (bf16[2048,768]{1,0:T(8,128)(2,1)S(1)}, f32[2048,768]{1,0:T(8,128)}, f32[2048,768]{1,0:T(8,128)}) fusion(f32[768]{0:T(1024)S(1)} %copy-done.118, bf16[768,768]{1,0:T(8,128)(2,1)S(1)} %copy-done, f32[768]{0:T(1024)S(1)} %copy-done.107, f32[768]{0:T(1024)S(1)} %copy-done.75, f32[2048]{0:T(1024)S(1)} %fusion.112, ...), kind=kOutput, calls=%fused_computation.44 | convolution fusion | flops 2533883904 | bytes 23228416 | tf_op jit(solution)/shard_map/dot_general | solution.py:101
  295.3 4.0 convolution_convert_fusion.1
  300.0 14.6 %psum.136 = f32[]{:T(128)} all-reduce(f32[]{:T(128)} %convert_reduce_fusion.4), channel_id=1, replica_groups=mesh['dp'=8,'tensor'=4] {'dp'}, use_global_device_ids=true, to_apply=%region_17.18 | all-reduce | flops 1 | bytes 8 | tf_op jit(solution)/shard_map/psum | solution.py:111
  315.3 104.2 %all-reduce.12.cloned.1.call-done = bf16[2048,768]{1,0:T(8,128)(2,1)} async-done(((bf16[2048,768]{1,0:T(8,128)(2,1)}), bf16[2048,768]{1,0:T(8,128)(2,1)}) %all-reduce.12.cloned.1.call-update) | async-done | bytes 3145744 | tf_op jit(solution)/shard_map/psum | solution.py:105
  419.5 5.2 fusion.138
  425.7 8.2 multiply_reduce_fusion.2
  433.9 3.4 fusion.137
  439.4 8.4 convert_reduce_fusion.1
  449.6 4.0 convolution_convert_fusion
  454.4 119.4 %all-reduce.14.cloned.1.call-done = bf16[2048,768]{1,0:T(8,128)(2,1)} async-done(((bf16[2048,768]{1,0:T(8,128)(2,1)}), bf16[2048,768]{1,0:T(8,128)(2,1)}) %all-reduce.14.cloned.1.call-update) | async-done | bytes 3145744 | tf_op jit(solution)/shard_map/psum | solution.py:124
  573.8 10.1 multiply_reduce_fusion.3
  583.9 6.0 fusion.136
  606.3 9.1 reshape.827
  615.5 5.2 multiply_reduce_fusion.1
  627.5 7.4 copy.64
  634.9 10.8 %multiply_reduce_fusion = (f32[3,512]{1,0:T(4,128)S(1)}, f32[3,512,2048]{2,1,0:T(8,128)}) fusion(f32[3,512,2048]{2,1,0:T(8,128)} %copy-done.2, f32[3,512]{1,0:T(4,128)S(1)} %log_add_fusion, bf16[512,3,64]{0,2,1:T(8,128)(2,1)S(1)} %bitcast.203, f32[2048,3,64]{0,2,1:T(8,128)S(1)} %bitcast.187, f32[3,64]{1,0:T(4,128)S(1)} %copy-done.74), kind=kOutput, calls=%fused_computation.1 | convolution fusion | flops 412875264 | bytes 26948352 | tf_op jit(solution)/shard_map/qhd,khd->hqk/dot_general | solution.py:149
  647.6 6.3 multiply_convert_fusion
  659.3 15.4 %reshape.829 = f32[3,512,4,512]{3,2,1,0:T(4,128)} reshape(bf16[3,512,2048]{2,1,0:T(8,128)(2,1)} %copy-done.5) | data formatting | bytes 18874368 | tf_op jit(solution)/shard_map/convert_element_type | solution.py:154
  674.7 11.9 %reduce_sum.323 = f32[3,512,512]{2,1,0:T(8,128)} reduce(f32[3,512,2,512]{3,2,1,0:T(2,128)} %reshape.827, f32[]{:T(128)} %constant.386.clone.1), dimensions={2}, to_apply=%region_48.49 | reduce | flops 786432 | bytes 9437188 | tf_op jit(solution)/shard_map/reduce_sum | solution.py:154
  686.6 3.5 copy.63
  690.1 7.0 reduce_sum.324
  697.1 12.7 %reduce_sum.325 = f32[3,512,512]{2,1,0:T(8,128)} reduce(f32[3,512,4,512]{3,2,1,0:T(4,128)} %reshape.829, f32[]{:T(128)} %constant.386.clone.1), dimensions={2}, to_apply=%region_50.51 | reduce | flops 2359296 | bytes 15728644 | tf_op jit(solution)/shard_map/reduce_sum | solution.py:154
  709.8 3.7 copy.65
  713.5 11.1 %fusion.30 = (f32[3,512,512]{1,2,0:T(8,128)}, bf16[3,512,512]{1,2,0:T(8,128)(2,1)S(1)}) fusion(f32[3,512,512]{1,2,0:T(8,128)} %copy.65, f32[3,512,512]{1,2,0:T(8,128)} %reduce_sum.324, f32[3,512,512]{1,2,0:T(8,128)} %copy.63, f32[3,512,512]{1,2,0:T(8,128)} %copy.54, f32[3,512,512]{1,2,0:T(8,128)} %copy.55, f32[3,512,512]{1,2,0:T(8,128)} %get-tuple-element.244, ...), kind=kLoop, calls=%fused_computation.86 | loop fusion | flops 20447232 | bytes 26750976 | tf_op jit(solution)/shard_map/transpose(jvp())/div | solution.py:75
  737.3 4.1 bitcast_convert_fusion
  741.8 7.1 fusion.148
  748.9 4.8 fusion.129
  755.4 3.2 fusion.70
  760.0 26.0 %all-reduce.2 = (f32[]{:T(128)}, f32[2,192]{1,0:T(2,128)}, f32[768]{0:T(1024)}, f32[768]{0:T(1024)}, f32[768]{0:T(1024)}, /*index=5*/f32[768]{0:T(1024)}, f32[768]{0:T(1024)}, f32[768]{0:T(1024)}, f32[768]{0:T(1024)}) all-reduce(f32[]{:T(128)} %get-tuple-element.182, ...), channel_id=1, replica_groups=mesh['dp'=8,'tensor'=4] {'dp'}, use_global_device_ids=true, to_apply=%region_15.16 | all-reduce | flops 5761 | bytes 46088 | tf_op jit(solution)/shard_map/psum | solution.py:111
  786.6 75.0 %all-reduce.16.cloned.1.call-done = bf16[2048,768]{1,0:T(8,128)(2,1)} async-done(((bf16[2048,768]{1,0:T(8,128)(2,1)}), bf16[2048,768]{1,0:T(8,128)(2,1)}) %all-reduce.16.cloned.1.call-update) | async-done | bytes 3145744 | tf_op jit(solution)/shard_map/psum | solution.py:187
  861.6 7.1 convert_add_fusion
  868.7 143.7 %all-reduce.18.cloned.1.call-done = (f32[3,768,192]{1,2,0:T(8,128)}, f32[192,768]{1,0:T(8,128)}, f32[768,768]{1,0:T(8,128)}, f32[768,768]{1,0:T(8,128)}, f32[3,512,512]{1,2,0:T(8,128)}) async-done(((f32[3,768,192]{1,2,0:T(8,128)}, f32[192,768]{1,0:T(8,128)}, f32[768,768]{1,0:T(8,128)}, f32[768,768]{1,0:T(8,128)}, f32[3,512,512]{1,2,0:T(8,128)}), (f32[3,768,192]{1,2,0:T(8,128)}, f32[192,768]{1,0:T(8,128)}, ...) | async-done | bytes 10223632 | tf_op jit(solution)/shard_map/psum | solution.py:191
  1012.4 3.7 copy.66
  (408 shorter events, 112.9 us)
Async XLA Ops:
  7.2 267.7 %copy-start = (bf16[768,768]{1,0:T(8,128)(2,1)S(1)}, bf16[768,768]{1,0:T(8,128)(2,1)}, u32[]{:S(2)}) copy-start(bf16[768,768]{1,0:T(8,128)(2,1)} %param.46) | copy-start | bytes 3538948
  7.2 261.2 %all-reduce.10.cloned.1.call-start = ((), (), s32[]{:S(2)}) async-start(), calls=%async_computation | async-start | bytes 6291456 | tf_op jit(solution)/shard_map/psum | solution.py:98
  19.4 106.7 %copy-start.19 = (bf16[1,2048,192]{1,2,0:T(8,128)(2,1)}, bf16[1,2048,192]{1,2,0:T(8,128)(2,1)S(1)}, u32[]{:S(2)}) copy-start(bf16[1,2048,192]{1,2,0:T(8,128)(2,1)S(1)} %slice.312) | copy-start | bytes 2359300
  26.7 108.1 %copy-start.73 = (f32[3,64]{1,0:T(4,128)}, f32[3,64]{1,0:T(4,128)S(1)}, u32[]{:S(2)}) copy-start(f32[3,64]{1,0:T(4,128)S(1)} %add.308) | copy-start | bytes 2308
  140.8 127.7 %copy-start.61 = (f32[768]{0:T(1024)S(1)}, f32[768]{0:T(1024)}, u32[]{:S(2)}) copy-start(f32[768]{0:T(1024)} %param.43) | copy-start | bytes 9220
  144.5 130.4 %copy-start.75 = (f32[768]{0:T(1024)S(1)}, f32[768]{0:T(1024)}, u32[]{:S(2)}) copy-start(f32[768]{0:T(1024)} %param.44) | copy-start | bytes 9220
  144.5 130.4 %copy-start.107 = (f32[768]{0:T(1024)S(1)}, f32[768]{0:T(1024)}, u32[]{:S(2)}) copy-start(f32[768]{0:T(1024)} %param.45) | copy-start | bytes 9220
  144.5 130.4 %copy-start.118 = (f32[768]{0:T(1024)S(1)}, f32[768]{0:T(1024)}, u32[]{:S(2)}) copy-start(f32[768]{0:T(1024)} %param.47) | copy-start | bytes 9220
  144.5 275.0 %all-reduce.12.cloned.1.call-start = ((), (), s32[]{:S(2)}) async-start(), calls=%async_computation.1 | async-start | bytes 6291456 | tf_op jit(solution)/shard_map/psum | solution.py:105
  274.9 309.0 %copy-start.54 = (f32[2048]{0:T(1024)}, f32[2048]{0:T(1024)S(1)}, u32[]{:S(2)}) copy-start(f32[2048]{0:T(1024)S(1)} %fusion.112) | copy-start | bytes 24580
  274.9 20.4 %copy-start.115 = (bf16[768,768]{1,0:T(8,128)(2,1)S(1)}, bf16[768,768]{1,0:T(8,128)(2,1)}, u32[]{:S(2)}) copy-start(bf16[768,768]{1,0:T(8,128)(2,1)} %param.48) | copy-start | bytes 3538948
  295.3 124.2 %copy-start.105 = (f32[768]{0:T(1024)S(1)}, f32[768]{0:T(1024)}, u32[]{:S(2)}) copy-start(f32[768]{0:T(1024)} %param.49) | copy-start | bytes 9220
  299.3 274.5 %all-reduce.14.cloned.1.call-start = ((), (), s32[]{:S(2)}) async-start(), calls=%async_computation.2 | async-start | bytes 6291456 | tf_op jit(solution)/shard_map/psum | solution.py:124
  437.3 10.6 %copy-start.6 = (f32[2048,768]{1,0:T(8,128)}, f32[2048,768]{1,0:T(8,128)S(1)}, u32[]{:S(2)}) copy-start(f32[2048,768]{1,0:T(8,128)S(1)} %get-tuple-element.208) | copy-start | bytes 18874372
  438.5 9.4 copy-start.30
  453.6 408.0 %all-reduce.16.cloned.1.call-start = ((), (), s32[]{:S(2)}) async-start(), calls=%async_computation.3 | async-start | bytes 6291456 | tf_op jit(solution)/shard_map/psum | solution.py:187
  453.7 142.7 %copy-start.59 = (f32[3,512]{1,0:T(4,128)}, f32[3,512]{1,0:T(4,128)S(1)}, u32[]{:S(2)}) copy-start(f32[3,512]{1,0:T(4,128)S(1)} %log_add_fusion.3) | copy-start | bytes 18436
  454.4 147.1 %copy-start.57 = (f32[3,512]{1,0:T(4,128)}, f32[3,512]{1,0:T(4,128)S(1)}, u32[]{:S(2)}) copy-start(f32[3,512]{1,0:T(4,128)S(1)} %log_add_fusion.2) | copy-start | bytes 18436
  573.8 10.1 copy-start.8
  573.8 10.1 copy-start.11
  573.8 10.1 copy-start.23
  591.6 7.9 copy-start.21
  591.6 7.9 slice-start.12
  604.6 10.9 %copy-start.32 = (bf16[1536,192]{0,1:T(8,128)(2,1)S(1)}, bf16[1536,192]{0,1:T(8,128)(2,1)}, u32[]{:S(2)}) copy-start(bf16[1536,192]{0,1:T(8,128)(2,1)} %slice.289) | copy-start | bytes 1769476
  604.6 10.9 %copy-start.56 = (f32[3,512]{1,0:T(4,128)S(1)}, f32[3,512]{1,0:T(4,128)}, u32[]{:S(2)}) copy-start(f32[3,512]{1,0:T(4,128)} %log_add_fusion.1) | copy-start | bytes 18436
  627.5 7.4 copy-start.74
  634.9 10.8 %slice-start = ((s8[12582912]{0:T(1024)(128)(4,1)}), s8[4194304]{0:T(1024)(128)(4,1)S(1)}, s32[]{:S(2)}) async-start(s8[12582912]{0:T(1024)(128)(4,1)} %bitcast.160), calls=%async_computation.5 | async-start | bytes 8388608
  634.9 10.8 %slice-start.1 = ((s8[12582912]{0:T(1024)(128)(4,1)}), s8[4194304]{0:T(1024)(128)(4,1)S(1)}, s32[]{:S(2)}) async-start(s8[12582912]{0:T(1024)(128)(4,1)} %bitcast.160), calls=%async_computation.6 | async-start | bytes 8388608
  634.9 12.6 %slice-start.2 = ((s8[12582912]{0:T(1024)(128)(4,1)}), s8[4194304]{0:T(1024)(128)(4,1)S(1)}, s32[]{:S(2)}) async-start(s8[12582912]{0:T(1024)(128)(4,1)} %bitcast.160), calls=%async_computation.7 | async-start | bytes 8388608
  647.6 9.0 copy-start.20
  713.5 12.3 %slice-start.14 = ((s8[6291456]{0:T(1024)(128)(4,1)}), s8[4194304]{0:T(1024)(128)(4,1)S(1)}, s32[]{:S(2)}) async-start(s8[6291456]{0:T(1024)(128)(4,1)} %bitcast.170), calls=%async_computation.19 | async-start | bytes 8388608
  713.5 11.1 %copy-start.42 = (bf16[1,512,192]{1,2,0:T(8,128)(2,1)S(1)}, bf16[1,512,192]{1,2,0:T(8,128)(2,1)}, u32[]{:S(2)}) copy-start(bf16[1,512,192]{1,2,0:T(8,128)(2,1)} %slice.285) | copy-start | bytes 589828
  713.5 11.5 %copy-start.41 = (bf16[512,192]{0,1:T(8,128)(2,1)S(1)}, bf16[512,192]{0,1:T(8,128)(2,1)}, u32[]{:S(2)}) copy-start(bf16[512,192]{0,1:T(8,128)(2,1)} %get-tuple-element.221) | copy-start | bytes 589828
  713.5 12.1 %copy-start.45 = (f32[512,3,64]{0,2,1:T(8,128)S(1)}, f32[512,3,64]{0,2,1:T(8,128)}, u32[]{:S(2)}) copy-start(f32[512,3,64]{0,2,1:T(8,128)} %fusion.85) | copy-start | bytes 1179652
  713.5 12.3 %slice-start.15 = ((s8[6291456]{0:T(1024)(128)(4,1)}), s8[2097152]{0:T(1024)(128)(4,1)S(1)}, s32[]{:S(2)}) async-start(s8[6291456]{0:T(1024)(128)(4,1)} %bitcast.170), calls=%async_computation.20 | async-start | bytes 4194304
  713.5 12.3 %copy-start.58 = (f32[3,512]{1,0:T(4,128)S(1)}, f32[3,512]{1,0:T(4,128)}, u32[]{:S(2)}) copy-start(f32[3,512]{1,0:T(4,128)} %copy-done.57) | copy-start | bytes 18436
  713.5 13.6 %slice-start.9 = ((s8[9437184]{0:T(1024)(128)(4,1)}), s8[4194304]{0:T(1024)(128)(4,1)S(1)}, s32[]{:S(2)}) async-start(s8[9437184]{0:T(1024)(128)(4,1)} %bitcast.166), calls=%async_computation.14 | async-start | bytes 8388608
  713.5 13.6 %slice-start.10 = ((s8[9437184]{0:T(1024)(128)(4,1)}), s8[4194304]{0:T(1024)(128)(4,1)S(1)}, s32[]{:S(2)}) async-start(s8[9437184]{0:T(1024)(128)(4,1)} %bitcast.166), calls=%async_computation.15 | async-start | bytes 8388608
  741.4 7.4 copy-start.55
  741.4 7.4 copy-start.62
  741.4 7.4 copy-start.76
  741.4 7.4 copy-start.108
  741.4 271.0 %all-reduce.18.cloned.1.call-start = ((), (), s32[]{:S(2)}) async-start(), calls=%async_computation.4 | async-start | bytes 20447232 | tf_op jit(solution)/shard_map/psum | solution.py:191
  741.7 7.1 copy-start.9
  741.8 7.1 copy-start.12
  758.6 103.0 %copy-start.64 = (f32[2048]{0:T(1024)S(1)}, f32[2048]{0:T(1024)}, u32[]{:S(2)}) copy-start(f32[2048]{0:T(1024)} %copy-done.63) | copy-start | bytes 24580
  1012.4 8.6 copy-start.34
  1016.1 7.7 copy-start.1
  (106 other events, 357.0 us)
Sparse Core Ops, SparseCore 0:
  144.6 123.7 all-reduce.9
  299.4 120.0 all-reduce.11
  453.7 120.0 all-reduce.13
  741.5 120.0 all-reduce.15
  867.0 145.3 all-reduce.17
where the time goes:
time: 1040 us; the launch traced here: 1030 us
  waiting for transfers between devices  566 us (54%)
  local copies, waits for them, and re-layouts  153 us (15%)
  other arithmetic  127 us (12%)
  matrix products  126 us (12%)
  blocking collectives  40.6 us (4%)
  between operations  19.2 us (2%)
    psum x1, waiting for transfers between devices, body(): lax.psum((grad_w_qkv, grad_b_qv, grad_w_attn_out, grad_b_attn_out, grad_g...  144 us
    psum x1, waiting for transfers between devices, body(): lax.psum(attn_part.astype(jnp.bfloat16), 'tensor').astype(jnp.float32)  124 us
    psum x1, waiting for transfers between devices, body(): lax.psum(back_first.astype(jnp.bfloat16), 'tensor').astype(jnp.float32)  119 us
    psum x1, waiting for transfers between devices, body(): lax.psum(ffn_part.astype(jnp.bfloat16), 'tensor').astype(jnp.float32)  104 us
    psum x1, waiting for transfers between devices, body(): lax.psum(back_hidden.astype(jnp.bfloat16), 'tensor').astype(jnp.float32)  75 us
    another operation x6, local copies, waits for them, and re-layouts, block_scores(): scores = scores + jnp.tile(gate_natural_log, (1, 1, block_index + 1))  56 us
    unnamed x305, local copies, waits for them, and re-layouts  45.1 us
    psum x2, blocking collectives, body(): total_valid, total_error = lax.psum((local_count, local_error), 'dp')  40.6 us
  transfers between devices with their start and end apart: 5, of which 5 were waited for; matrix products, arithmetic and copies ran while one was open for 2% of the time, Pallas kernels for 0%

commit v1 on v0

--- a/solution.py
+++ b/solution.py
@@ -7,6 +7,11 @@
 BLOCK = 256
 epsilon = 1e-06
 gumbel_softening_factor = 0.5
+
+
+def summed_here(block, name):
+    parts = lax.all_gather(block, name)
+    return jnp.sum(parts, axis=0)
 
 
 def normed(resid, gain, shift):
@@ -102,7 +107,7 @@
     activated, gelu_pull = jax.vjp(exact_gelu, before)
     act_low = activated.astype(jnp.bfloat16)
     ffn_part = jnp.dot(act_low, w_down, preferred_element_type=jnp.float32)
-    feedforward = lax.psum(ffn_part.astype(jnp.bfloat16), "tensor").astype(jnp.float32) + b_down
+    feedforward = summed_here(ffn_part.astype(jnp.bfloat16), "tensor").astype(jnp.float32) + b_down
     out_states, second_pull = jax.vjp(normed, first + feedforward, gain_two, bias_two)
     valid_rows = valid[0].astype(jnp.float32)[:, None]
     residue = out_states - teacher

time: 1040 us -> 1150 us (1.11)
  waiting for transfers between devices: 566 us -> 663 us
    all_gather x0 -> x1, waiting for transfers between devices: none -> 202 us  [summed_here(): parts = lax.all_gather(block, name)]
    psum x1 -> x0, waiting for transfers between devices: 104 us -> none  [body(): lax.psum(ffn_part.astype(jnp.bfloat16), 'tensor').astype(jnp.float32)]
where the time goes in v1:
time: 1150 us; the launch traced here: 1140 us
  waiting for transfers between devices  663 us (58%)
  local copies, waits for them, and re-layouts  153 us (13%)
  other arithmetic  136 us (12%)
  matrix products  126 us (11%)
  blocking collectives  40.2 us (3%)
  between operations  19.2 us (2%)
    all_gather x1, waiting for transfers between devices, summed_here(): parts = lax.all_gather(block, name)  202 us
    psum x1, waiting for transfers between devices, body(): lax.psum((grad_w_qkv, grad_b_qv, grad_w_attn_out, grad_b_attn_out, grad_g...  144 us
    psum x1, waiting for transfers between devices, body(): lax.psum(attn_part.astype(jnp.bfloat16), 'tensor').astype(jnp.float32)  124 us
    psum x1, waiting for transfers between devices, body(): lax.psum(back_first.astype(jnp.bfloat16), 'tensor').astype(jnp.float32)  119 us
    psum x1, waiting for transfers between devices, body(): lax.psum(back_hidden.astype(jnp.bfloat16), 'tensor').astype(jnp.float32)  75 us
    another operation x6, local copies, waits for them, and re-layouts, block_scores(): scores = scores + jnp.tile(gate_natural_log, (1, 1, block_index + 1))  56 us
    unnamed x305, local copies, waits for them, and re-layouts  45.2 us
    psum x2, blocking collectives, body(): total_valid, total_error = lax.psum((local_count, local_error), 'dp')  40.2 us
  transfers between devices with their start and end apart: 5, of which 5 were waited for; matrix products, arithmetic and copies ran while one was open for 2% of the time, Pallas kernels for 0%

profile of v1, /device:TPU:0, one launch (start us, length us, event | category | flops | bytes accessed | tf_op | source)
XLA Modules:
  0.0 1137.1 jit_solution(2344270272187298622)
XLA Ops:
  15.1 4.2 convolution_bitcast_fusion
  26.7 3.5 copy.54
  30.2 3.6 copy.55
  33.8 6.4 fusion.35
  40.2 3.6 copy.57
  46.0 7.0 tile.14
  53.0 9.6 copy.58
  62.6 6.6 tile.12
  69.1 9.2 tile.13
  78.3 7.7 tile.16
  86.1 15.9 %tile.17 = f32[3,512,2048]{2,1,0:T(8,128)} reshape(f32[3,512,4,512]{3,2,1,0:T(4,128)} %tile.16) | data formatting | bytes 25165824 | tf_op jit(solution)/shard_map/tile | solution.py:39
  126.1 6.7 fusion.143
  137.5 3.2 fusion.97
  144.6 123.8 %all-reduce.9.cloned.1.call-done = bf16[2048,768]{1,0:T(8,128)(2,1)} async-done(((bf16[2048,768]{1,0:T(8,128)(2,1)}), bf16[2048,768]{1,0:T(8,128)(2,1)}) %all-reduce.9.cloned.1.call-update) | async-done | bytes 3145744 | tf_op jit(solution)/shard_map/psum | solution.py:103
  268.4 4.1 fusion.17
  274.9 18.6 %multiply_convert_fusion.3 = (bf16[2048,768]{1,0:T(8,128)(2,1)S(1)}, f32[2048,768]{1,0:T(8,128)}, f32[2048,768]{1,0:T(8,128)}) fusion(f32[768]{0:T(1024)S(1)} %copy-done.118, bf16[768,768]{1,0:T(8,128)(2,1)S(1)} %copy-done, f32[768]{0:T(1024)S(1)} %copy-done.107, f32[768]{0:T(1024)S(1)} %copy-done.75, f32[2048]{0:T(1024)S(1)} %fusion.112, ...), kind=kOutput, calls=%fused_computation.44 | convolution fusion | flops 2533883904 | bytes 23228416 | tf_op jit(solution)/shard_map/dot_general | solution.py:106
  295.3 3.9 convolution_convert_fusion.1
  300.0 14.2 %psum.128 = f32[]{:T(128)} all-reduce(f32[]{:T(128)} %convert_reduce_fusion.4), channel_id=1, replica_groups=mesh['dp'=8,'tensor'=4] {'dp'}, use_global_device_ids=true, to_apply=%region_17.18 | all-reduce | flops 1 | bytes 8 | tf_op jit(solution)/shard_map/psum | solution.py:116
  314.9 201.7 %all-gather.3.cloned.1.call-done = bf16[8192,768]{1,0:T(8,128)(2,1)} async-done(((bf16[2048,768]{1,0:T(8,128)(2,1)}), bf16[8192,768]{1,0:T(8,128)(2,1)}) %all-gather.3.cloned.1.call-update) | async-done | bytes 12582928 | tf_op jit(solution)/shard_map/all_gather | solution.py:13
  516.7 9.0 reduce_sum.315
  525.6 5.2 fusion.138
  531.8 8.2 multiply_reduce_fusion.2
  540.0 3.4 fusion.137
  545.5 8.4 convert_reduce_fusion.1
  555.6 4.0 convolution_convert_fusion
  560.5 118.6 %all-reduce.11.cloned.1.call-done = bf16[2048,768]{1,0:T(8,128)(2,1)} async-done(((bf16[2048,768]{1,0:T(8,128)(2,1)}), bf16[2048,768]{1,0:T(8,128)(2,1)}) %all-reduce.11.cloned.1.call-update) | async-done | bytes 3145744 | tf_op jit(solution)/shard_map/psum | solution.py:129
  679.1 10.1 multiply_reduce_fusion.3
  689.2 6.0 fusion.136
  711.6 9.1 reshape.827
  720.7 5.2 multiply_reduce_fusion.1
  732.8 7.4 copy.64
  740.2 10.8 multiply_reduce_fusion
  752.8 6.3 multiply_convert_fusion
  764.6 15.4 %reshape.829 = f32[3,512,4,512]{3,2,1,0:T(4,128)} reshape(bf16[3,512,2048]{2,1,0:T(8,128)(2,1)} %copy-done.5) | data formatting | bytes 18874368 | tf_op jit(solution)/shard_map/convert_element_type | solution.py:159
  780.0 11.9 %reduce_sum.336 = f32[3,512,512]{2,1,0:T(8,128)} reduce(f32[3,512,2,512]{3,2,1,0:T(2,128)} %reshape.827, f32[]{:T(128)} %constant.387.clone.1), dimensions={2}, to_apply=%region_48.49 | reduce | flops 786432 | bytes 9437188 | tf_op jit(solution)/shard_map/reduce_sum | solution.py:159
  791.8 3.5 copy.63
  795.4 7.0 reduce_sum.337
  802.4 12.7 %reduce_sum.338 = f32[3,512,512]{2,1,0:T(8,128)} reduce(f32[3,512,4,512]{3,2,1,0:T(4,128)} %reshape.829, f32[]{:T(128)} %constant.387.clone.1), dimensions={2}, to_apply=%region_50.51 | reduce | flops 2359296 | bytes 15728644 | tf_op jit(solution)/shard_map/reduce_sum | solution.py:159
  815.0 3.7 copy.65
  818.8 11.1 fusion.30
  842.6 4.1 bitcast_convert_fusion
  847.0 7.1 fusion.148
  854.2 4.8 fusion.129
  865.2 26.0 %all-reduce.2 = (f32[]{:T(128)}, f32[2,192]{1,0:T(2,128)}, f32[768]{0:T(1024)}, f32[768]{0:T(1024)}, f32[768]{0:T(1024)}, /*index=5*/f32[768]{0:T(1024)}, f32[768]{0:T(1024)}, f32[768]{0:T(1024)}, f32[768]{0:T(1024)}) all-reduce(f32[]{:T(128)} %get-tuple-element.182, ...), channel_id=1, replica_groups=mesh['dp'=8,'tensor'=4] {'dp'}, use_global_device_ids=true, to_apply=%region_15.16 | all-reduce | flops 5761 | bytes 46088 | tf_op jit(solution)/shard_map/psum | solution.py:116
  891.9 75.0 %all-reduce.13.cloned.1.call-done = bf16[2048,768]{1,0:T(8,128)(2,1)} async-done(((bf16[2048,768]{1,0:T(8,128)(2,1)}), bf16[2048,768]{1,0:T(8,128)(2,1)}) %all-reduce.13.cloned.1.call-update) | async-done | bytes 3145744 | tf_op jit(solution)/shard_map/psum | solution.py:192
  966.9 7.1 convert_add_fusion
  974.0 143.7 %all-reduce.15.cloned.1.call-done = (f32[3,768,192]{1,2,0:T(8,128)}, f32[192,768]{1,0:T(8,128)}, f32[768,768]{1,0:T(8,128)}, f32[768,768]{1,0:T(8,128)}, f32[3,512,512]{1,2,0:T(8,128)}) async-done(((f32[3,768,192]{1,2,0:T(8,128)}, f32[192,768]{1,0:T(8,128)}, f32[768,768]{1,0:T(8,128)}, f32[768,768]{1,0:T(8,128)}, f32[3,512,512]{1,2,0:T(8,128)}), (f32[3,768,192]{1,2,0:T(8,128)}, f32[192,768]{1,0:T(8,128)}, ...) | async-done | bytes 10223632 | tf_op jit(solution)/shard_map/psum | solution.py:196
  1117.7 3.7 copy.66
  (409 shorter events, 116.1 us)
Async XLA Ops:
  7.2 267.7 %copy-start = (bf16[768,768]{1,0:T(8,128)(2,1)S(1)}, bf16[768,768]{1,0:T(8,128)(2,1)}, u32[]{:S(2)}) copy-start(bf16[768,768]{1,0:T(8,128)(2,1)} %param.46) | copy-start | bytes 3538948
  7.2 261.2 %all-reduce.9.cloned.1.call-start = ((), (), s32[]{:S(2)}) async-start(), calls=%async_computation | async-start | bytes 6291456 | tf_op jit(solution)/shard_map/psum | solution.py:103
  19.4 106.7 %copy-start.19 = (bf16[1,2048,192]{1,2,0:T(8,128)(2,1)}, bf16[1,2048,192]{1,2,0:T(8,128)(2,1)S(1)}, u32[]{:S(2)}) copy-start(bf16[1,2048,192]{1,2,0:T(8,128)(2,1)S(1)} %slice.312) | copy-start | bytes 2359300
  26.7 108.1 %copy-start.73 = (f32[3,64]{1,0:T(4,128)}, f32[3,64]{1,0:T(4,128)S(1)}, u32[]{:S(2)}) copy-start(f32[3,64]{1,0:T(4,128)S(1)} %add.306) | copy-start | bytes 2308
  140.8 127.7 %copy-start.61 = (f32[768]{0:T(1024)S(1)}, f32[768]{0:T(1024)}, u32[]{:S(2)}) copy-start(f32[768]{0:T(1024)} %param.43) | copy-start | bytes 9220
  144.5 130.4 %copy-start.75 = (f32[768]{0:T(1024)S(1)}, f32[768]{0:T(1024)}, u32[]{:S(2)}) copy-start(f32[768]{0:T(1024)} %param.44) | copy-start | bytes 9220
  144.5 130.4 %copy-start.107 = (f32[768]{0:T(1024)S(1)}, f32[768]{0:T(1024)}, u32[]{:S(2)}) copy-start(f32[768]{0:T(1024)} %param.45) | copy-start | bytes 9220
  144.5 130.4 %copy-start.118 = (f32[768]{0:T(1024)S(1)}, f32[768]{0:T(1024)}, u32[]{:S(2)}) copy-start(f32[768]{0:T(1024)} %param.47) | copy-start | bytes 9220
  144.5 372.1 %all-gather.3.cloned.1.call-start = ((), (), s32[]{:S(2)}) async-start(), calls=%async_computation.3 | async-start | bytes 15728640 | tf_op jit(solution)/shard_map/all_gather | solution.py:13
  274.9 414.3 %copy-start.54 = (f32[2048]{0:T(1024)}, f32[2048]{0:T(1024)S(1)}, u32[]{:S(2)}) copy-start(f32[2048]{0:T(1024)S(1)} %fusion.112) | copy-start | bytes 24580
  274.9 20.4 %copy-start.115 = (bf16[768,768]{1,0:T(8,128)(2,1)S(1)}, bf16[768,768]{1,0:T(8,128)(2,1)}, u32[]{:S(2)}) copy-start(bf16[768,768]{1,0:T(8,128)(2,1)} %param.48) | copy-start | bytes 3538948
  299.3 379.8 %all-reduce.11.cloned.1.call-start = ((), (), s32[]{:S(2)}) async-start(), calls=%async_computation.1 | async-start | bytes 6291456 | tf_op jit(solution)/shard_map/psum | solution.py:129
  516.6 9.0 copy-start.105
  543.4 10.6 copy-start.6
  544.6 9.4 copy-start.30
  559.7 407.2 %all-reduce.13.cloned.1.call-start = ((), (), s32[]{:S(2)}) async-start(), calls=%async_computation.2 | async-start | bytes 6291456 | tf_op jit(solution)/shard_map/psum | solution.py:192
  559.8 141.9 %copy-start.59 = (f32[3,512]{1,0:T(4,128)}, f32[3,512]{1,0:T(4,128)S(1)}, u32[]{:S(2)}) copy-start(f32[3,512]{1,0:T(4,128)S(1)} %log_add_fusion.3) | copy-start | bytes 18436
  560.4 146.3 %copy-start.57 = (f32[3,512]{1,0:T(4,128)}, f32[3,512]{1,0:T(4,128)S(1)}, u32[]{:S(2)}) copy-start(f32[3,512]{1,0:T(4,128)S(1)} %log_add_fusion.2) | copy-start | bytes 18436
  679.1 10.1 copy-start.8
  679.1 10.1 copy-start.11
  679.1 10.1 copy-start.23
  696.9 7.9 copy-start.21
  696.9 7.9 slice-start.12
  709.8 10.9 copy-start.32
  709.8 10.9 copy-start.56
  732.8 7.4 copy-start.74
  740.2 10.8 slice-start
  740.2 10.8 slice-start.1
  740.2 12.6 %slice-start.2 = ((s8[12582912]{0:T(1024)(128)(4,1)}), s8[4194304]{0:T(1024)(128)(4,1)S(1)}, s32[]{:S(2)}) async-start(s8[12582912]{0:T(1024)(128)(4,1)} %bitcast.161), calls=%async_computation.7 | async-start | bytes 8388608
  752.8 9.0 copy-start.20
  818.7 12.3 %slice-start.14 = ((s8[6291456]{0:T(1024)(128)(4,1)}), s8[4194304]{0:T(1024)(128)(4,1)S(1)}, s32[]{:S(2)}) async-start(s8[6291456]{0:T(1024)(128)(4,1)} %bitcast.171), calls=%async_computation.19 | async-start | bytes 8388608
  818.7 11.1 copy-start.42
  818.7 11.5 %copy-start.41 = (bf16[512,192]{0,1:T(8,128)(2,1)S(1)}, bf16[512,192]{0,1:T(8,128)(2,1)}, u32[]{:S(2)}) copy-start(bf16[512,192]{0,1:T(8,128)(2,1)} %get-tuple-element.221) | copy-start | bytes 589828
  818.8 12.1 %copy-start.45 = (f32[512,3,64]{0,2,1:T(8,128)S(1)}, f32[512,3,64]{0,2,1:T(8,128)}, u32[]{:S(2)}) copy-start(f32[512,3,64]{0,2,1:T(8,128)} %fusion.85) | copy-start | bytes 1179652
  818.8 12.3 %slice-start.15 = ((s8[6291456]{0:T(1024)(128)(4,1)}), s8[2097152]{0:T(1024)(128)(4,1)S(1)}, s32[]{:S(2)}) async-start(s8[6291456]{0:T(1024)(128)(4,1)} %bitcast.171), calls=%async_computation.20 | async-start | bytes 4194304
  818.8 12.3 %copy-start.58 = (f32[3,512]{1,0:T(4,128)S(1)}, f32[3,512]{1,0:T(4,128)}, u32[]{:S(2)}) copy-start(f32[3,512]{1,0:T(4,128)} %copy-done.57) | copy-start | bytes 18436
  818.8 13.6 %slice-start.9 = ((s8[9437184]{0:T(1024)(128)(4,1)}), s8[4194304]{0:T(1024)(128)(4,1)S(1)}, s32[]{:S(2)}) async-start(s8[9437184]{0:T(1024)(128)(4,1)} %bitcast.167), calls=%async_computation.14 | async-start | bytes 8388608
  818.8 13.6 %slice-start.10 = ((s8[9437184]{0:T(1024)(128)(4,1)}), s8[4194304]{0:T(1024)(128)(4,1)S(1)}, s32[]{:S(2)}) async-start(s8[9437184]{0:T(1024)(128)(4,1)} %bitcast.167), calls=%async_computation.15 | async-start | bytes 8388608
  846.7 7.4 copy-start.55
  846.7 7.4 copy-start.62
  846.7 7.4 copy-start.76
  846.7 7.4 copy-start.108
  846.7 270.9 %all-reduce.15.cloned.1.call-start = ((), (), s32[]{:S(2)}) async-start(), calls=%async_computation.4 | async-start | bytes 20447232 | tf_op jit(solution)/shard_map/psum | solution.py:196
  847.0 7.1 copy-start.9
  847.0 7.1 copy-start.12
  863.9 103.0 %copy-start.64 = (f32[2048]{0:T(1024)S(1)}, f32[2048]{0:T(1024)}, u32[]{:S(2)}) copy-start(f32[2048]{0:T(1024)} %copy-done.63) | copy-start | bytes 24580
  1117.7 8.6 copy-start.34
  1121.4 7.7 copy-start.1
  (106 other events, 356.9 us)
Sparse Core Ops, SparseCore 0:
  144.6 123.7 all-reduce.8
  299.4 217.1 all-gather.2
  559.8 119.2 all-reduce.10
  846.8 120.0 all-reduce.12
  972.3 145.3 all-reduce.14
